TPU v7x, 128 devices: a whole 4x4x4 slice. The times are simulated.
128 devices in a mesh: seq: 128 (over x, z, y, core).
Axes of the slice: x: 4, y: 4, z: 4, core: 2. Of those that a mesh axis runs over, the one named last changes fastest.
Arguments:
- activations: bfloat16 [262144, 384], P('seq'), may hold values from -6 to 6
- conv_weight: bfloat16 [4, 3, 384, 384], replicated, may hold values from -0.1875 to 0.1875
- conv_bias: float32 [4, 384], replicated, may hold values from -3 to 3
- conv_gain: float32 [4, 384], replicated, may hold values from 0.1 to 1.9
- mlp_gain: float32 [4, 384], replicated, may hold values from 0.1 to 1.9
- w_in: bfloat16 [4, 384, 768], replicated, may hold values from -0.3125 to 0.3125
- w_out: bfloat16 [4, 768, 384], replicated, may hold values from -0.21875 to 0.21875
Outputs:
- channel_major: bfloat16 [384, 262144], P('seq')
All inputs are finite; a program needn't handle non-finite values.
Results may differ from a plain program's by a relative error of at most 0.015.
Values may be sent and summed in bfloat16 or wider, within the bound.
A program may use at most 64 MiB of HBM per device.

v0:
```python
import jax
import jax.numpy as jnp
from jax import lax
from jax.sharding import PartitionSpec as P


def from_behind(block, axis, distance):
    devices = range(lax.axis_size(axis))
    route = [(i - distance, i) for i in devices if i - distance in devices]
    return lax.ppermute(block, axis, route)


def rms_scale(values, gain):
    wide = values.astype(jnp.float32)
    inverse = lax.rsqrt(jnp.mean(wide * wide, axis=-1, keepdims=True) + 1e-06)
    return (wide * inverse * gain[None, :]).astype(jnp.bfloat16)


def one_layer(state, taps, bias, gain_conv, gain_mlp, proj_in, proj_out, distance):
    normed = rms_scale(state, gain_conv)
    earlier = from_behind(normed, "seq", distance)
    later = from_behind(normed, "seq", -distance)
    pre = jnp.dot(normed, taps[1], preferred_element_type=jnp.float32)
    pre = pre + jnp.dot(earlier, taps[0], preferred_element_type=jnp.float32)
    pre = pre + jnp.dot(later, taps[2], preferred_element_type=jnp.float32)
    pre = pre + bias[None, :]
    middle = (state.astype(jnp.float32) + jax.nn.gelu(pre, approximate=False)).astype(jnp.bfloat16)
    inner = rms_scale(middle, gain_mlp)
    hidden = jax.nn.gelu(
        jnp.dot(inner, proj_in, preferred_element_type=jnp.float32), approximate=False
    ).astype(jnp.bfloat16)
    return (
        middle.astype(jnp.float32) + jnp.dot(hidden, proj_out, preferred_element_type=jnp.float32)
    ).astype(jnp.bfloat16)


def shards(activations, conv_weight, conv_bias, conv_gain, mlp_gain, w_in, w_out):
    state = activations
    for layer in range(conv_weight.shape[0]):
        state = one_layer(
            state,
            conv_weight[layer],
            conv_bias[layer],
            conv_gain[layer],
            mlp_gain[layer],
            w_in[layer],
            w_out[layer],
            2**layer,
        )
    return lax.all_to_all(state.T, "seq", split_axis=0, concat_axis=1, tiled=True)


def solution(mesh):
    in_specs = (P("seq", None), P(), P(), P(), P(), P(), P())
    out_specs = P("seq", None)
    return jax.shard_map(shards, mesh=mesh, in_specs=in_specs, out_specs=out_specs, check_vma=False)
```

profile of v0, /device:TPU:1, one launch (start us, length us, event | category | flops | bytes accessed | tf_op | source)
XLA Modules:
  0.0 358.9 jit_solution(2985881944252996278)
XLA Ops:
  0.0 1.5 slice_reduce_fusion.2
  1.5 1.7 copy.10
  3.2 0.0 copy-start.4
  3.2 0.0 copy-start.5
  3.2 0.3 fusion.40
  3.5 0.4 fusion.42
  4.0 4.6 %collective-permute-start = (bf16[2048,384]{0,1:T(8,128)(2,1)S(1)}, bf16[2048,384]{0,1:T(8,128)(2,1)S(1)}, u32[]{:S(2)}, u32[]{:S(2)}) collective-permute-start(bf16[2048,384]{0,1:T(8,128)(2,1)S(1)} %fusion.42), channel_id=1, source_target_pairs={{0,1},{1,2},{2,3},{3,4},{4,5},{5,6},{6,7},{7,8},{8,9},{9,10},{10,1... | collective-permute-start | bytes 4718600 | tf_op jit(solution)/shard_map/ppermute | solution.py:10
  8.5 1.9 collective-permute-start.1
  10.5 0.0 copy-done.4
  10.5 0.6 slice_reduce_fusion.1
  11.1 0.0 copy-done.5
  11.1 0.6 slice_reduce_fusion
  11.7 2.0 fusion.201
  13.7 12.2 %collective-permute-done = bf16[2048,384]{0,1:T(8,128)(2,1)S(1)} collective-permute-done((bf16[2048,384]{0,1:T(8,128)(2,1)S(1)}, bf16[2048,384]{0,1:T(8,128)(2,1)S(1)}, u32[]{:S(2)}, u32[]{:S(2)}) %collective-permute-start) | collective-permute-done | bytes 1572896 | tf_op jit(solution)/shard_map/ppermute | solution.py:10
  25.9 2.0 fusion.199
  27.9 2.4 collective-permute-done.1
  30.3 10.5 %fusion.46 = (f32[2048]{0:T(1024)S(1)}, bf16[2048,384]{0,1:T(8,128)(2,1)}) fusion(f32[384]{0:T(512)S(1)} %get-tuple-element.11, bf16[2048,384]{0,1:T(8,128)(2,1)S(1)} %collective-permute-done.1, bf16[4,3,384,384]{3,2,1,0:T(8,128)(2,1)} %param.8, f32[2048,384]{0,1:T(8,128)S(1)} %fusion.201, f32[2048,384]{0,1:T(8,128)S(1)} %fusion.199, ...), kind=kOutput, calls=%fused_computation.110 | convolution fusion | flops 661387264 | bytes 11314688 | tf_op jit(solution)/shard_map/dot_general | solution.py:25
  40.8 0.0 copy-start
  40.8 20.1 %fusion.50 = (f32[2048]{0:T(1024)S(1)}, bf16[2048,384]{0,1:T(8,128)(2,1)}) fusion(bf16[4,768,384]{2,1,0:T(8,128)(2,1)} %param.13, bf16[2048,384]{0,1:T(8,128)(2,1)} %get-tuple-element.18, f32[384]{0:T(512)} %get-tuple-element.7, f32[2048]{0:T(1024)S(1)} %add_rsqrt_fusion.6, bf16[4,384,768]{2,1,0:T(8,128)(2,1)} %param.12), kind=kOutput, calls=%fused_computation.114 | convolution fusion | flops 2526017536 | bytes 5916672 | tf_op jit(solution)/shard_map/dot_general | solution.py:33
  60.9 1.8 fusion.52
  62.7 3.3 collective-permute-start.2
  66.0 1.3 collective-permute-start.3
  67.3 0.0 copy-done
  67.3 1.0 fusion.196
  68.4 0.0 copy-start.2
  68.4 0.0 copy-start.9
  68.4 31.1 %collective-permute-done.2 = bf16[2048,384]{0,1:T(8,128)(2,1)S(1)} collective-permute-done((bf16[2048,384]{0,1:T(8,128)(2,1)S(1)}, bf16[2048,384]{0,1:T(8,128)(2,1)S(1)}, u32[]{:S(2)}, u32[]{:S(2)}) %collective-permute-start.2) | collective-permute-done | bytes 1572896 | tf_op jit(solution)/shard_map/ppermute | solution.py:10
  99.5 1.0 fusion.194
  100.5 3.2 collective-permute-done.3
  103.7 0.0 copy-done.2
  103.7 0.0 copy-done.9
  103.7 9.5 %fusion.56 = (f32[2048]{0:T(1024)S(1)}, bf16[2048,384]{0,1:T(8,128)(2,1)}) fusion(f32[384]{0:T(512)S(1)} %copy-done.9, bf16[2048,384]{0,1:T(8,128)(2,1)S(1)} %collective-permute-done.3, bf16[4,3,384,384]{3,2,1,0:T(8,128)(2,1)S(1)} %copy-done, f32[2048,384]{0,1:T(8,128)S(1)} %fusion.196, f32[2048,384]{0,1:T(8,128)S(1)} %fusion.194, ...), kind=kOutput, calls=%fused_computation.120 | convolution fusion | flops 661387264 | bytes 11315200 | tf_op jit(solution)/shard_map/dot_general | solution.py:25
  113.2 19.7 %fusion.60 = (f32[2048]{0:T(1024)S(1)}, bf16[2048,384]{0,1:T(8,128)(2,1)}) fusion(bf16[4,768,384]{2,1,0:T(8,128)(2,1)} %param.13, bf16[2048,384]{0,1:T(8,128)(2,1)} %get-tuple-element.22, f32[384]{0:T(512)} %get-tuple-element.6, f32[2048]{0:T(1024)S(1)} %add_rsqrt_fusion.4, bf16[4,384,768]{2,1,0:T(8,128)(2,1)} %param.12), kind=kOutput, calls=%fused_computation.124 | convolution fusion | flops 2526017536 | bytes 5916672 | tf_op jit(solution)/shard_map/dot_general | solution.py:33
  132.9 1.8 fusion.62
  134.7 6.2 %collective-permute-start.4 = (bf16[2048,384]{0,1:T(8,128)(2,1)S(1)}, bf16[2048,384]{0,1:T(8,128)(2,1)S(1)}, u32[]{:S(2)}, u32[]{:S(2)}) collective-permute-start(bf16[2048,384]{0,1:T(8,128)(2,1)S(1)} %fusion.62), channel_id=1, source_target_pairs={{0,4},{1,5},{2,6},{3,7},{4,8},{5,9},{6,10},{7,11},{8,12},{9,13},{1... | collective-permute-start | bytes 4718600 | tf_op jit(solution)/shard_map/ppermute | solution.py:10
  140.9 1.3 collective-permute-start.5
  142.2 1.0 fusion.191
  143.3 0.0 copy-start.3
  143.3 0.0 copy-start.8
  143.3 65.1 %collective-permute-done.4 = bf16[2048,384]{0,1:T(8,128)(2,1)S(1)} collective-permute-done((bf16[2048,384]{0,1:T(8,128)(2,1)S(1)}, bf16[2048,384]{0,1:T(8,128)(2,1)S(1)}, u32[]{:S(2)}, u32[]{:S(2)}) %collective-permute-start.4) | collective-permute-done | bytes 1572896 | tf_op jit(solution)/shard_map/ppermute | solution.py:10
  208.3 1.0 fusion.189
  209.4 0.0 collective-permute-done.5
  209.4 0.0 copy-done.3
  209.4 0.0 copy-done.8
  209.4 9.5 %fusion.66 = (f32[2048]{0:T(1024)S(1)}, bf16[2048,384]{0,1:T(8,128)(2,1)}) fusion(f32[384]{0:T(512)S(1)} %copy-done.8, bf16[2048,384]{0,1:T(8,128)(2,1)S(1)} %collective-permute-done.5, bf16[4,3,384,384]{3,2,1,0:T(8,128)(2,1)S(1)} %copy-done, f32[2048,384]{0,1:T(8,128)S(1)} %fusion.191, f32[2048,384]{0,1:T(8,128)S(1)} %fusion.189, ...), kind=kOutput, calls=%fused_computation.130 | convolution fusion | flops 661387264 | bytes 11315200 | tf_op jit(solution)/shard_map/dot_general | solution.py:25
  218.9 19.8 %fusion.70 = (f32[2048]{0:T(1024)S(1)}, bf16[2048,384]{0,1:T(8,128)(2,1)}) fusion(bf16[4,768,384]{2,1,0:T(8,128)(2,1)} %param.13, bf16[2048,384]{0,1:T(8,128)(2,1)} %get-tuple-element.26, f32[384]{0:T(512)} %get-tuple-element.8, f32[2048]{0:T(1024)S(1)} %add_rsqrt_fusion.2, bf16[4,384,768]{2,1,0:T(8,128)(2,1)} %param.12), kind=kOutput, calls=%fused_computation.134 | convolution fusion | flops 2526017536 | bytes 5916672 | tf_op jit(solution)/shard_map/dot_general | solution.py:33
  238.7 1.8 fusion.72
  240.5 2.8 collective-permute-start.6
  243.3 1.3 collective-permute-start.7
  244.6 1.0 fusion.186
  245.6 0.0 copy-start.1
  245.6 0.0 copy-start.7
  245.6 29.2 %collective-permute-done.6 = bf16[2048,384]{0,1:T(8,128)(2,1)S(1)} collective-permute-done((bf16[2048,384]{0,1:T(8,128)(2,1)S(1)}, bf16[2048,384]{0,1:T(8,128)(2,1)S(1)}, u32[]{:S(2)}, u32[]{:S(2)}) %collective-permute-start.6) | collective-permute-done | bytes 1572896 | tf_op jit(solution)/shard_map/ppermute | solution.py:10
  274.9 1.0 fusion.184
  275.9 2.9 collective-permute-done.7
  278.8 0.0 copy-done.1
  278.8 0.0 copy-done.7
  278.8 0.0 copy-start.6
  278.8 9.5 %fusion.76 = (f32[2048]{0:T(1024)S(1)}, bf16[2048,384]{0,1:T(8,128)(2,1)}) fusion(f32[384]{0:T(512)S(1)} %copy-done.7, bf16[2048,384]{0,1:T(8,128)(2,1)S(1)} %collective-permute-done.7, bf16[4,3,384,384]{3,2,1,0:T(8,128)(2,1)S(1)} %copy-done, f32[2048,384]{0,1:T(8,128)S(1)} %fusion.186, f32[2048,384]{0,1:T(8,128)S(1)} %fusion.184, ...), kind=kOutput, calls=%fused_computation.140 | convolution fusion | flops 661387264 | bytes 11315200 | tf_op jit(solution)/shard_map/dot_general | solution.py:25
  288.3 0.0 copy-done.6
  288.3 19.5 %fusion.124 = bf16[384,2048]{1,0:T(8,128)(2,1)} fusion(bf16[2048,384]{0,1:T(8,128)(2,1)} %get-tuple-element.30, f32[384]{0:T(512)S(1)} %copy-done.6, f32[2048]{0:T(1024)S(1)} %add_rsqrt_fusion, bf16[4,768,384]{2,1,0:T(8,128)(2,1)} %param.13, bf16[4,384,768]{2,1,0:T(8,128)(2,1)} %param.12), kind=kOutput, calls=%fused_computation.212 | convolution fusion | flops 2523660288 | bytes 5907968 | tf_op jit(solution)/shard_map/dot_general | solution.py:33
  307.9 4.0 %all_to_all.14 = bf16[128,3,2048]{2,1,0:T(4,128)(2,1)S(1)} reshape(bf16[384,2048]{1,0:T(8,128)(2,1)} %fusion.124) | data formatting | bytes 3145728 | tf_op jit(solution)/shard_map/all_to_all | solution.py:50
  311.9 45.4 %all_to_all.19 = bf16[128,3,2048]{2,1,0:T(4,128)(2,1)S(1)} all-to-all(bf16[128,3,2048]{2,1,0:T(4,128)(2,1)S(1)} %all_to_all.14), channel_id=1, replica_groups=mesh['seq'=128] {'seq'}, dimensions={0} | all-to-all | bytes 3145728 | tf_op jit(solution)/shard_map/all_to_all | solution.py:50
  357.3 1.3 copy.12
  (8 shorter events, 0.1 us)
Async XLA Ops:
  3.2 7.3 %copy-start.4 = (f32[4,384]{1,0:T(4,128)S(1)}, f32[4,384]{1,0:T(4,128)}, u32[]{:S(2)}) copy-start(f32[4,384]{1,0:T(4,128)} %param.9) | copy-start | bytes 18436
  3.2 7.9 %copy-start.5 = (f32[4,384]{1,0:T(4,128)S(1)}, f32[4,384]{1,0:T(4,128)}, u32[]{:S(2)}) copy-start(f32[4,384]{1,0:T(4,128)} %param.11) | copy-start | bytes 18436
  4.0 21.9 %collective-permute-start = (bf16[2048,384]{0,1:T(8,128)(2,1)S(1)}, bf16[2048,384]{0,1:T(8,128)(2,1)S(1)}, u32[]{:S(2)}, u32[]{:S(2)}) collective-permute-start(bf16[2048,384]{0,1:T(8,128)(2,1)S(1)} %fusion.42), channel_id=1, source_target_pairs={{0,1},{1,2},{2,3},{3,4},{4,5},{5,6},{6,7},{7,8},{8,9},{9,10},{10,1... | collective-permute-start | bytes 4718600 | tf_op jit(solution)/shard_map/ppermute | solution.py:10
  8.5 21.7 %collective-permute-start.1 = (bf16[2048,384]{0,1:T(8,128)(2,1)S(1)}, bf16[2048,384]{0,1:T(8,128)(2,1)S(1)}, u32[]{:S(2)}, u32[]{:S(2)}) collective-permute-start(bf16[2048,384]{0,1:T(8,128)(2,1)S(1)} %fusion.42), channel_id=1, source_target_pairs={{1,0},{2,1},{3,2},{4,3},{5,4},{6,5},{7,6},{8,7},{9,8},{10,9},{11,1... | collective-permute-start | bytes 4718600 | tf_op jit(solution)/shard_map/ppermute | solution.py:10
  40.8 26.5 %copy-start = (bf16[4,3,384,384]{3,2,1,0:T(8,128)(2,1)S(1)}, bf16[4,3,384,384]{3,2,1,0:T(8,128)(2,1)}, u32[]{:S(2)}) copy-start(bf16[4,3,384,384]{3,2,1,0:T(8,128)(2,1)} %param.8) | copy-start | bytes 10616836
  62.7 36.8 %collective-permute-start.2 = (bf16[2048,384]{0,1:T(8,128)(2,1)S(1)}, bf16[2048,384]{0,1:T(8,128)(2,1)S(1)}, u32[]{:S(2)}, u32[]{:S(2)}) collective-permute-start(bf16[2048,384]{0,1:T(8,128)(2,1)S(1)} %fusion.52), channel_id=1, source_target_pairs={{0,2},{1,3},{2,4},{3,5},{4,6},{5,7},{6,8},{7,9},{8,10},{9,11},{10,... | collective-permute-start | bytes 4718600 | tf_op jit(solution)/shard_map/ppermute | solution.py:10
  66.0 37.7 %collective-permute-start.3 = (bf16[2048,384]{0,1:T(8,128)(2,1)S(1)}, bf16[2048,384]{0,1:T(8,128)(2,1)S(1)}, u32[]{:S(2)}, u32[]{:S(2)}) collective-permute-start(bf16[2048,384]{0,1:T(8,128)(2,1)S(1)} %fusion.52), channel_id=1, source_target_pairs={{2,0},{3,1},{4,2},{5,3},{6,4},{7,5},{8,6},{9,7},{10,8},{11,9},{12,... | collective-permute-start | bytes 4718600 | tf_op jit(solution)/shard_map/ppermute | solution.py:10
  68.4 35.3 %copy-start.2 = (bf16[2048,384]{0,1:T(8,128)(2,1)S(1)}, bf16[2048,384]{0,1:T(8,128)(2,1)}, u32[]{:S(2)}) copy-start(bf16[2048,384]{0,1:T(8,128)(2,1)} %get-tuple-element.20) | copy-start | bytes 4718596
  68.4 35.3 %copy-start.9 = (f32[384]{0:T(512)S(1)}, f32[384]{0:T(512)}, u32[]{:S(2)}) copy-start(f32[384]{0:T(512)} %get-tuple-element.10) | copy-start | bytes 4612
  134.7 73.6 %collective-permute-start.4 = (bf16[2048,384]{0,1:T(8,128)(2,1)S(1)}, bf16[2048,384]{0,1:T(8,128)(2,1)S(1)}, u32[]{:S(2)}, u32[]{:S(2)}) collective-permute-start(bf16[2048,384]{0,1:T(8,128)(2,1)S(1)} %fusion.62), channel_id=1, source_target_pairs={{0,4},{1,5},{2,6},{3,7},{4,8},{5,9},{6,10},{7,11},{8,12},{9,13},{1... | collective-permute-start | bytes 4718600 | tf_op jit(solution)/shard_map/ppermute | solution.py:10
  140.9 68.5 %collective-permute-start.5 = (bf16[2048,384]{0,1:T(8,128)(2,1)S(1)}, bf16[2048,384]{0,1:T(8,128)(2,1)S(1)}, u32[]{:S(2)}, u32[]{:S(2)}) collective-permute-start(bf16[2048,384]{0,1:T(8,128)(2,1)S(1)} %fusion.62), channel_id=1, source_target_pairs={{4,0},{5,1},{6,2},{7,3},{8,4},{9,5},{10,6},{11,7},{12,8},{13,9},{1... | collective-permute-start | bytes 4718600 | tf_op jit(solution)/shard_map/ppermute | solution.py:10
  143.3 66.1 %copy-start.3 = (bf16[2048,384]{0,1:T(8,128)(2,1)S(1)}, bf16[2048,384]{0,1:T(8,128)(2,1)}, u32[]{:S(2)}) copy-start(bf16[2048,384]{0,1:T(8,128)(2,1)} %get-tuple-element.24) | copy-start | bytes 4718596
  143.3 66.1 %copy-start.8 = (f32[384]{0:T(512)S(1)}, f32[384]{0:T(512)}, u32[]{:S(2)}) copy-start(f32[384]{0:T(512)} %get-tuple-element.12) | copy-start | bytes 4612
  240.5 34.4 %collective-permute-start.6 = (bf16[2048,384]{0,1:T(8,128)(2,1)S(1)}, bf16[2048,384]{0,1:T(8,128)(2,1)S(1)}, u32[]{:S(2)}, u32[]{:S(2)}) collective-permute-start(bf16[2048,384]{0,1:T(8,128)(2,1)S(1)} %fusion.72), channel_id=1, source_target_pairs={{0,8},{1,9},{2,10},{3,11},{4,12},{5,13},{6,14},{7,15},{8,16},{9,17... | collective-permute-start | bytes 4718600 | tf_op jit(solution)/shard_map/ppermute | solution.py:10
  243.3 35.5 %collective-permute-start.7 = (bf16[2048,384]{0,1:T(8,128)(2,1)S(1)}, bf16[2048,384]{0,1:T(8,128)(2,1)S(1)}, u32[]{:S(2)}, u32[]{:S(2)}) collective-permute-start(bf16[2048,384]{0,1:T(8,128)(2,1)S(1)} %fusion.72), channel_id=1, source_target_pairs={{8,0},{9,1},{10,2},{11,3},{12,4},{13,5},{14,6},{15,7},{16,8},{17,9... | collective-permute-start | bytes 4718600 | tf_op jit(solution)/shard_map/ppermute | solution.py:10
  245.6 33.2 %copy-start.1 = (bf16[2048,384]{0,1:T(8,128)(2,1)S(1)}, bf16[2048,384]{0,1:T(8,128)(2,1)}, u32[]{:S(2)}) copy-start(bf16[2048,384]{0,1:T(8,128)(2,1)} %get-tuple-element.28) | copy-start | bytes 4718596
  245.6 33.2 %copy-start.7 = (f32[384]{0:T(512)S(1)}, f32[384]{0:T(512)}, u32[]{:S(2)}) copy-start(f32[384]{0:T(512)} %get-tuple-element.9) | copy-start | bytes 4612
  278.8 9.5 %copy-start.6 = (f32[384]{0:T(512)S(1)}, f32[384]{0:T(512)}, u32[]{:S(2)}) copy-start(f32[384]{0:T(512)} %get-tuple-element.5) | copy-start | bytes 4612
where the time goes:
time: 363 us; the launch traced here: 359 us
  waiting for transfers between devices  146 us (40%)
  matrix products  128 us (35%)
  blocking collectives  45.4 us (13%)
  starting transfers between devices  22.7 us (6%)
  local copies, waits for them, and re-layouts  9.77 us (3%)
  other arithmetic  6.2 us (2%)
    ppermute x8, waiting for transfers between devices, from_behind(): return lax.ppermute(block, axis, route)  146 us
    dot_general x4, matrix products, one_layer(): jnp.dot(hidden, proj_out, preferred_element_type=jnp.float32)  79.1 us
    all_to_all x1, blocking collectives, shards(): lax.all_to_all(state.T, 'seq', split_axis=0, concat_axis=1, tiled=True)  45.4 us
    dot_general x4, matrix products, one_layer(): pre = pre + jnp.dot(later, taps[2], preferred_element_type=jnp.float32)  38.9 us
    ppermute x8, starting transfers between devices, from_behind(): return lax.ppermute(block, axis, route)  22.7 us
  transfers between devices with their start and end apart: 8, of which 7 were waited for; matrix products, arithmetic and copies ran while one was open for 3% of the time, Pallas kernels for 0%

commit v1 on v0

v1 whole, which is shorter than its diff:
```python
import functools
import jax
import jax.numpy as jnp
from jax import lax
from jax.experimental import pallas as pl
from jax.experimental.pallas import tpu as pltpu
from jax.sharding import PartitionSpec as P

PAD = 8


def gelu(x):
    half = 0.5 * x
    return half + half * lax.erf(x * 0.7071067811865476)


def rms(wide, gain):
    inverse = lax.rsqrt(jnp.mean(wide * wide, axis=-1, keepdims=True) + 1e-06)
    return (wide * inverse * gain).astype(jnp.bfloat16)


def tower(state, normed, flat, packed, cw, cb, cg, mg, wi, wo, G, TB):
    nb, _, ch = state.shape
    layers = cw.shape[0]
    tiles = nb // TB

    def fill_pads(buf, d_blocks):
        if G == 16:
            zero = jnp.zeros((PAD, 16, ch), jnp.bfloat16)
            normed[buf, pl.ds(0, PAD)] = zero
            normed[buf, pl.ds(PAD + nb, PAD)] = zero
        else:
            tail = normed[buf, pl.ds(nb, PAD)].astype(jnp.float32)
            head = normed[buf, pl.ds(PAD, PAD)].astype(jnp.float32)
            zero = jnp.zeros((PAD, G, ch), jnp.float32)
            normed[buf, pl.ds(0, PAD)] = jnp.concatenate([zero, tail[:, : 16 - G]], axis=1).astype(jnp.bfloat16)
            normed[buf, pl.ds(PAD + nb, PAD)] = jnp.concatenate([head[:, G:], zero], axis=1).astype(jnp.bfloat16)

    def first(t, _):
        x = state[pl.ds(t * TB, TB)].reshape(TB * 16, ch).astype(jnp.float32)
        normed[0, pl.ds(PAD + t * TB, TB)] = rms(x, cg[0, :][None, :]).reshape(TB, 16, ch)
        return 0

    lax.fori_loop(0, tiles, first, 0)
    fill_pads(0, 1)

    def body(layer, t, last):
        cur = lax.rem(layer, 2)
        d = lax.shift_left(1, layer)
        b0 = PAD + t * TB
        lhs = jnp.concatenate(
            [normed[cur, pl.ds(b0 + s, TB)].reshape(TB * 16, ch) for s in (-d, 0, d)], axis=1
        )
        pre = jnp.dot(lhs, cw[layer], preferred_element_type=jnp.float32) + cb[layer, :][None, :]
        x = state[pl.ds(t * TB, TB)].reshape(TB * 16, ch).astype(jnp.float32)
        middle = (x + gelu(pre)).astype(jnp.bfloat16)
        wide = middle.astype(jnp.float32)
        inner = rms(wide, mg[layer, :][None, :])
        hidden = gelu(jnp.dot(inner, wi[layer], preferred_element_type=jnp.float32)).astype(jnp.bfloat16)
        out = wide + jnp.dot(hidden, wo[layer], preferred_element_type=jnp.float32)
        if last:
            for k in range(3):
                flat[k, pl.ds(t * TB * 16, TB * 16)] = out[:, k * 128 : (k + 1) * 128]
        else:
            new = out.astype(jnp.bfloat16)
            state[pl.ds(t * TB, TB)] = new.reshape(TB, 16, ch)
            normed[1 - cur, pl.ds(b0, TB)] = rms(new.astype(jnp.float32), cg[layer + 1, :][None, :]).reshape(TB, 16, ch)
        return 0

    def one_layer(layer, _):
        lax.fori_loop(0, tiles, lambda t, c: body(layer, t, False), 0)
        fill_pads(1 - lax.rem(layer, 2), 0)
        return 0

    lax.fori_loop(0, layers - 1, one_layer, 0)
    lax.fori_loop(0, tiles, lambda t, c: body(layers - 1, t, True), 0)


def emit(flat, turned, packed, G):
    nb = flat.shape[1] // 16
    for k in range(3):
        for o in range(G):
            rows = [flat[k, pl.ds(f * G + o, nb, stride=16), :] for f in range(16 // G)]
            block = rows[0] if len(rows) == 1 else jnp.concatenate(rows, axis=0)
            turned[pl.ds(k * 128 * G + o, 128, stride=G), :] = block.T
    n = packed.shape[0]
    step = 8

    def cast(g, _):
        values = turned[pl.ds(pl.multiple_of(g * step * 3 * G, 8), step * 3 * G), :]
        packed[pl.ds(g * step, step)] = values.astype(jnp.bfloat16).reshape(step, 3 * G, 128)
        return 0

    lax.fori_loop(0, n // step, cast, 0)


def kernel(x_hbm, cw_hbm, cb, cg, mg, wi_hbm, wo_hbm, out_ref, state, normed, flat, turned, cw, wi, wo, sem, *, G, TB):
    loads = [
        pltpu.make_async_copy(s, d, sem.at[n])
        for n, (s, d) in enumerate(((x_hbm, state), (cw_hbm, cw), (wi_hbm, wi), (wo_hbm, wo)))
    ]
    for load in loads:
        load.start()
    for load in loads:
        load.wait()
    tower(state, normed, flat, None, cw, cb, cg, mg, wi, wo, G, TB)
    emit(flat, turned, out_ref, G)


def shards(activations, conv_weight, conv_bias, conv_gain, mlp_gain, w_in, w_out):
    n = lax.axis_size("seq")
    rows, ch = activations.shape
    layers = conv_weight.shape[0]
    hid = w_in.shape[2]
    G = rows // n
    taps = conv_weight.reshape(layers, 3 * ch, ch)
    mine = lax.all_to_all(activations, "seq", split_axis=0, concat_axis=0, tiled=True)
    vm = pl.BlockSpec(memory_space=pltpu.VMEM)
    hbm = pl.BlockSpec(memory_space=pl.ANY)
    packed = pl.pallas_call(
        functools.partial(kernel, G=G, TB=16),
        out_shape=jax.ShapeDtypeStruct((n, 3 * G, n), jnp.bfloat16),
        in_specs=[hbm, hbm, vm, vm, vm, hbm, hbm],
        out_specs=vm,
        scratch_shapes=[
            pltpu.VMEM((n * G // 16, 16, ch), jnp.bfloat16),
            pltpu.VMEM((2, n * G // 16 + 2 * PAD, 16, ch), jnp.bfloat16),
            pltpu.VMEM((3, n * G, 128), jnp.float32),
            pltpu.VMEM((ch * G, 128), jnp.float32),
            pltpu.VMEM((layers, 3 * ch, ch), jnp.bfloat16),
            pltpu.VMEM((layers, ch, hid), jnp.bfloat16),
            pltpu.VMEM((layers, hid, ch), jnp.bfloat16),
            pltpu.SemaphoreType.DMA((4,)),
        ],
        compiler_params=pltpu.CompilerParams(vmem_limit_bytes=56 * 1024 * 1024),
    )(mine.reshape(n * G // 16, 16, ch), taps, conv_bias, conv_gain, mlp_gain, w_in, w_out)
    got = lax.all_to_all(packed, "seq", split_axis=0, concat_axis=0, tiled=True)
    return got.reshape(n, 3, G, n).transpose(1, 3, 0, 2).reshape(3, n * n * G)


def solution(mesh):
    in_specs = (P("seq", None), P(), P(), P(), P(), P(), P())
    out_specs = P("seq", None)
    return jax.shard_map(shards, mesh=mesh, in_specs=in_specs, out_specs=out_specs, check_vma=False)
```

time: 363 us -> 150 us (0.41)
  waiting for transfers between devices: 146 us -> 0 us
  matrix products: 128 us -> 0 us
  Pallas kernels: 0 us -> 50.9 us
  local copies, waits for them, and re-layouts: 9.77 us -> 32.7 us
  starting transfers between devices: 22.7 us -> 0 us
  blocking collectives: 45.4 us -> 65.8 us
  other arithmetic: 6.2 us -> 0 us
    ppermute x8 -> x0, waiting for transfers between devices: 146 us -> none  [from_behind(): return lax.ppermute(block, axis, route)]
    dot_general x16 -> x0, matrix products: 128 us -> none  [the longest x4 79.1 us: one_layer(): jnp.dot(hidden, proj_out, preferred_element_type=jnp.float32)]
    pallas_call x0 -> x1, Pallas kernels: none -> 50.9 us  [shards(): pl.pallas_call(functools.partial(kernel, G=G, TB=16), out_shape=jax.Shape...]
    ppermute x8 -> x0, starting transfers between devices: 22.7 us -> none  [from_behind(): return lax.ppermute(block, axis, route)]
    all_to_all x1 -> x2, blocking collectives: 45.4 us -> 65.8 us  [the longest x1 36.2 us: shards(): lax.all_to_all(activations, 'seq', split_axis=0, concat_axis=0, tiled=True)]
    reshape x0 -> x2, local copies, waits for them, and re-layouts: none -> 19.2 us  [shards(): return got.reshape(n, 3, G, n).transpose(1, 3, 0, 2).reshape(3, n * n * G)]
    unnamed x22 -> x1, local copies, waits for them, and re-layouts: 3.07 us -> 13.5 us
    convert_element_type x4 -> x0, other arithmetic: 5.81 us -> none  [rms_scale(): return (wide * inverse * gain[None, :]).astype(jnp.bfloat16)]
  transfers between devices with their start and end apart: 8 -> 0, of which waited for: 7 -> 0; matrix products, arithmetic and copies ran while one was open for 3% -> 0% of each run, Pallas kernels for 0% -> 0%
where the time goes in v1:
time: 150 us; the launch traced here: 149 us
  blocking collectives  65.8 us (44%)
  Pallas kernels  50.9 us (34%)
  local copies, waits for them, and re-layouts  32.7 us (22%)
    pallas_call x1, Pallas kernels, shards(): pl.pallas_call(functools.partial(kernel, G=G, TB=16), out_shape=jax.Shape...  50.9 us
    all_to_all x1, blocking collectives, shards(): lax.all_to_all(activations, 'seq', split_axis=0, concat_axis=0, tiled=True)  36.2 us
    all_to_all x1, blocking collectives, shards(): got = lax.all_to_all(packed, 'seq', split_axis=0, concat_axis=0, tiled=True)  29.7 us
    reshape x2, local copies, waits for them, and re-layouts, shards(): return got.reshape(n, 3, G, n).transpose(1, 3, 0, 2).reshape(3, n * n * G)  19.2 us
    unnamed x1, local copies, waits for them, and re-layouts  13.5 us

profile of v1, /device:TPU:1, one launch (start us, length us, event | category | flops | bytes accessed | tf_op | source)
XLA Modules:
  0.0 149.5 jit_solution(8118761813183151395)
XLA Ops:
  0.0 36.2 %all_to_all.14.x_hbm = bf16[128,16,384]{2,1,0:T(8,128)(2,1)} all-to-all(bf16[128,16,384]{2,1,0:T(8,128)(2,1)} %bitcast.9), channel_id=1, replica_groups=mesh['seq'=128] {'seq'}, dimensions={0} | all-to-all | bytes 3145728 | tf_op jit(solution)/shard_map/all_to_all | solution.py:117
  36.2 50.9 %shard_map.73 = bf16[128,48,128]{2,1,0:T(8,128)(2,1)} custom-call(bf16[128,16,384]{2,1,0:T(8,128)(2,1)} %all_to_all.14.x_hbm, bf16[4,1152,384]{2,1,0:T(8,128)(2,1)} %bitcast.8, f32[4,384]{1,0:T(4,128)} %cb.1, f32[4,384]{1,0:T(4,128)} %cg.1, f32[4,384]{1,0:T(4,128)} %mg.1, bf16[4,384,768]{2,1,0:T(8,128)(2,1)} %wi_hbm.1, bf16[4,768,384]{2,1,0:T(8,128)(2,1)} %wo_hbm.1), custom_call_target="tpu_custom_call" | custom-call | tf_op jit(solution)/shard_map/pallas_call | solution.py:120
  87.1 29.7 %all_to_all.15 = bf16[128,48,128]{2,1,0:T(8,128)(2,1)S(1)} all-to-all(bf16[128,48,128]{2,1,0:T(8,128)(2,1)} %shard_map.73), channel_id=1, replica_groups=mesh['seq'=128] {'seq'}, dimensions={0} | all-to-all | bytes 3145728 | tf_op jit(solution)/shard_map/all_to_all | solution.py:137
  116.8 17.2 %copy.9 = bf16[128,3,16,128]{2,0,3,1:T(8,128)(2,1)} copy(bf16[128,3,16,128]{3,2,1,0:T(8,128)(2,1)S(1)} %bitcast.7) | data formatting | bytes 3145728 | tf_op jit(solution)/shard_map/reshape | solution.py:138
  134.0 13.5 %reshape.16 = bf16[786432]{0:T(1024)(128)(2,1)S(1)} reshape(bf16[3,128,128,16]{3,2,1,0:T(8,128)(2,1)} %bitcast.6) | data formatting | bytes 3145728
  147.5 2.0 %reshape.15 = bf16[3,262144]{1,0:T(4,128)(2,1)} reshape(bf16[786432]{0:T(1024)(128)(2,1)S(1)} %reshape.16) | data formatting | bytes 3145728 | tf_op jit(solution)/shard_map/reshape | solution.py:138

commit v2 on v1

v2 whole, which is shorter than its diff:
```python
import functools

import jax
import jax.numpy as jnp
from jax import lax
from jax.experimental import pallas as pl
from jax.experimental.pallas import tpu as pltpu
from jax.sharding import PartitionSpec as P

PAD = 8
G = 8
SEG = 16 // G
TB = 16
STRIDE = 37
MESH = pl.DeviceIdType.MESH


def gelu(x):
    half = 0.5 * x
    return half + half * lax.erf(x * 0.7071067811865476)


def rms(wide, gain):
    inverse = lax.rsqrt(jnp.mean(wide * wide, axis=-1, keepdims=True) + 1e-06)
    return (wide * inverse * gain).astype(jnp.bfloat16)


def tower(c, state, normed, flat, cw, cb, cg, mg, wi, wo):
    nb, ch = state.shape[1], state.shape[-1]
    layers = cw.shape[0]
    tiles = nb // TB

    def rows_of(t):
        return state[c, pl.ds(t * TB, TB)].reshape(TB * 16, ch)

    def fill_pads(buf):
        tail = normed[buf, pl.ds(nb, PAD)].astype(jnp.float32)
        head = normed[buf, pl.ds(PAD, PAD)].astype(jnp.float32)
        zero = jnp.zeros((PAD, G, ch), jnp.float32)
        normed[buf, pl.ds(0, PAD)] = jnp.concatenate([zero, tail[:, : 16 - G]], axis=1).astype(jnp.bfloat16)
        normed[buf, pl.ds(PAD + nb, PAD)] = jnp.concatenate([head[:, G:], zero], axis=1).astype(jnp.bfloat16)

    def first(t, carry):
        x = rows_of(t).astype(jnp.float32)
        normed[0, pl.ds(PAD + t * TB, TB)] = rms(x, cg[0, :][None, :]).reshape(TB, 16, ch)
        return carry

    lax.fori_loop(0, tiles, first, 0)
    fill_pads(0)

    def body(layer, t, last):
        cur = lax.rem(layer, 2)
        d = lax.shift_left(1, layer)
        b0 = PAD + t * TB
        lhs = jnp.concatenate(
            [normed[cur, pl.ds(b0 + s, TB)].reshape(TB * 16, ch) for s in (-d, 0, d)], axis=1
        )
        pre = jnp.dot(lhs, cw[layer], preferred_element_type=jnp.float32) + cb[layer, :][None, :]
        middle = (rows_of(t).astype(jnp.float32) + gelu(pre)).astype(jnp.bfloat16)
        wide = middle.astype(jnp.float32)
        inner = rms(wide, mg[layer, :][None, :])
        hidden = gelu(jnp.dot(inner, wi[layer], preferred_element_type=jnp.float32)).astype(jnp.bfloat16)
        out = wide + jnp.dot(hidden, wo[layer], preferred_element_type=jnp.float32)
        if last:
            for k in range(ch // 128):
                flat[k, pl.ds(t * TB * 16, TB * 16)] = out[:, k * 128 : (k + 1) * 128]
        else:
            new = out.astype(jnp.bfloat16)
            state[c, pl.ds(t * TB, TB)] = new.reshape(TB, SEG, G, ch)
            scaled = rms(new.astype(jnp.float32), cg[layer + 1, :][None, :])
            normed[1 - cur, pl.ds(b0, TB)] = scaled.reshape(TB, 16, ch)
        return 0

    def one_layer(layer, carry):
        lax.fori_loop(0, tiles, lambda t, x: body(layer, t, False), 0)
        fill_pads(1 - lax.rem(layer, 2))
        return carry

    lax.fori_loop(0, layers - 1, one_layer, 0)
    lax.fori_loop(0, tiles, lambda t, x: body(layers - 1, t, True), 0)


def emit(c, flat, turned, packed):
    nb = flat.shape[1] // 16
    for k in range(flat.shape[0]):
        for o in range(G):
            rows = [flat[k, pl.ds(f * G + o, nb, stride=16), :] for f in range(SEG)]
            block = jnp.concatenate(rows, axis=0)
            turned[pl.ds(k * 128 * G + o, 128, stride=G), :] = block.T
    step, per = 8, packed.shape[2]

    def cast(g, carry):
        values = turned[pl.ds(pl.multiple_of(g * step * per, 8), step * per), :]
        packed[c, pl.ds(g * step, step)] = values.astype(jnp.bfloat16).reshape(step, per, 128)
        return carry

    lax.fori_loop(0, packed.shape[1] // step, cast, 0)


def move_kernel(
    x_hbm, cw_hbm, cb, cg, mg, wi_hbm, wo_hbm, got,
    state, normed, flat, turned, packed, cw, wi, wo,
    load_sem, in_send, in_recv, out_send, out_recv,
):
    me = lax.axis_index("seq")
    chunks, n = packed.shape[0], packed.shape[1]
    nb = state.shape[1]
    loads = [
        pltpu.make_async_copy(s, d, load_sem.at[k])
        for k, (s, d) in enumerate(((cw_hbm, cw), (wi_hbm, wi), (wo_hbm, wo)))
    ]
    for load in loads:
        load.start()

    def peer_of(q):
        p = lax.rem(q * STRIDE, n)
        core = lax.rem(me + p, 2)
        y = lax.rem(me // 2 + p // 2, 4)
        z = lax.rem(me // 8 + p // 8, 4)
        x = lax.rem(me // 32 + p // 32, 4)
        return ((x * 4 + z) * 4 + y) * 2 + core

    barrier = pltpu.get_barrier_semaphore()

    def greet(q, carry):
        pl.semaphore_signal(barrier, inc=1, device_id=(peer_of(q),), device_id_type=MESH)
        return carry

    lax.fori_loop(1, n, greet, 0)
    pl.semaphore_wait(barrier, n - 1)

    def source(c, j):
        return x_hbm.at[pl.ds(pl.multiple_of((c * n + j) * G, 8), G)]

    home = lax.rem(me, nb), me // nb
    for c in range(chunks):
        place = state.at[c, home[0], home[1]]
        pltpu.make_async_copy(source(c, me), place, in_recv.at[c]).start()

        def send(q, carry):
            j = peer_of(q)
            pltpu.make_async_remote_copy(
                source(c, j), place, in_send.at[c], in_recv.at[c], device_id=(j,), device_id_type=MESH
            ).start()
            return carry

        lax.fori_loop(1, n, send, 0)
    for load in loads:
        load.wait()

    def one_chunk(c, carry):
        pltpu.make_async_copy(state.at[c], state.at[c], in_recv.at[c]).wait()
        tower(c, state, normed, flat, cw, cb, cg, mg, wi, wo)
        emit(c, flat, turned, packed)
        pltpu.make_async_copy(packed.at[c, me], got.at[c, me], out_recv.at[c]).start()

        def send(q, x):
            j = peer_of(q)
            pltpu.make_async_remote_copy(
                packed.at[c, j], got.at[c, me], out_send.at[c], out_recv.at[c],
                device_id=(j,), device_id_type=MESH,
            ).start()
            return x

        lax.fori_loop(1, n, send, 0)
        return carry

    lax.fori_loop(0, chunks, one_chunk, 0)
    for c in range(chunks):
        sent = x_hbm.at[pl.ds(0, (n - 1) * G)]
        pltpu.make_async_copy(sent, sent, in_send.at[c]).wait()
        sent = packed.at[c, pl.ds(0, n - 1)]
        pltpu.make_async_copy(sent, sent, out_send.at[c]).wait()
        pltpu.make_async_copy(got.at[c], got.at[c], out_recv.at[c]).wait()


def turn_kernel(got, out_ref, wide):
    chunks, n = got.shape[0], got.shape[1]
    per = 128 // G
    blocks = n // per
    total = chunks * blocks
    for r in range(3):
        def one(b, carry):
            c, g = b // blocks, lax.rem(b, blocks)
            tile = got[c, pl.ds(g * per, per), pl.ds(r * G, G), :].reshape(128, n).astype(jnp.float32)
            wide[pl.ds(b * 4 + r, n, stride=4 * total), :] = tile.T
            return carry

        lax.fori_loop(0, total, one, 0)

    def store(i, carry):
        base = pl.multiple_of(i * total * 4, 4)
        row = jnp.concatenate([wide[pl.ds(base + 4 * b, 4), :] for b in range(total)], axis=1)
        out_ref[:, pl.ds(pl.multiple_of(i * total * 128, 128), total * 128)] = row[:3].astype(jnp.bfloat16)
        return carry

    lax.fori_loop(0, n, store, 0)


def shards(activations, conv_weight, conv_bias, conv_gain, mlp_gain, w_in, w_out):
    n = lax.axis_size("seq")
    rows, ch = activations.shape
    layers = conv_weight.shape[0]
    hid = w_in.shape[2]
    chunks = rows // (n * G)
    nb = n // SEG
    own = ch // n
    taps = conv_weight.reshape(layers, 3 * ch, ch)
    vm = pl.BlockSpec(memory_space=pltpu.VMEM)
    hbm = pl.BlockSpec(memory_space=pl.ANY)
    got = pl.pallas_call(
        move_kernel,
        out_shape=jax.ShapeDtypeStruct((chunks, n, own * G, n), jnp.bfloat16),
        in_specs=[hbm, hbm, vm, vm, vm, hbm, hbm],
        out_specs=hbm,
        scratch_shapes=[
            pltpu.VMEM((chunks, nb, SEG, G, ch), jnp.bfloat16),
            pltpu.VMEM((2, nb + 2 * PAD, 16, ch), jnp.bfloat16),
            pltpu.VMEM((ch // 128, n * G, 128), jnp.float32),
            pltpu.VMEM((ch * G, 128), jnp.float32),
            pltpu.VMEM((chunks, n, own * G, n), jnp.bfloat16),
            pltpu.VMEM((layers, 3 * ch, ch), jnp.bfloat16),
            pltpu.VMEM((layers, ch, hid), jnp.bfloat16),
            pltpu.VMEM((layers, hid, ch), jnp.bfloat16),
            pltpu.SemaphoreType.DMA((3,)),
            pltpu.SemaphoreType.DMA((chunks,)),
            pltpu.SemaphoreType.DMA((chunks,)),
            pltpu.SemaphoreType.DMA((chunks,)),
            pltpu.SemaphoreType.DMA((chunks,)),
        ],
        compiler_params=pltpu.CompilerParams(
            vmem_limit_bytes=40 * 1024 * 1024, collective_id=0, has_side_effects=True
        ),
    )(activations, taps, conv_bias, conv_gain, mlp_gain, w_in, w_out)
    return pl.pallas_call(
        turn_kernel,
        out_shape=jax.ShapeDtypeStruct((own, n * rows), jnp.bfloat16),
        in_specs=[vm],
        out_specs=vm,
        scratch_shapes=[pltpu.VMEM((n * rows // 128 * 4, 128), jnp.float32)],
        compiler_params=pltpu.CompilerParams(vmem_limit_bytes=40 * 1024 * 1024),
    )(got)


def solution(mesh):
    in_specs = (P("seq", None), P(), P(), P(), P(), P(), P())
    out_specs = P("seq", None)
    return jax.shard_map(shards, mesh=mesh, in_specs=in_specs, out_specs=out_specs, check_vma=False)
```

time: 150 us -> 109 us (0.73)
  blocking collectives: 65.8 us -> 0 us
  Pallas kernels: 50.9 us -> 100 us
  local copies, waits for them, and re-layouts: 32.7 us -> 8.81 us
    all_to_all x2 -> x0, blocking collectives: 65.8 us -> none  [the longest x1 36.2 us: shards(): lax.all_to_all(activations, 'seq', split_axis=0, concat_axis=0, tiled=True)]
    pallas_call x1 -> x2, Pallas kernels: 50.9 us -> 100 us  [the longest x1 90.8 us: shards(): pl.pallas_call(move_kernel, out_shape=jax.ShapeDtypeStruct((chunks, n, ow...]
    reshape x2 -> x0, local copies, waits for them, and re-layouts: 19.2 us -> none  [shards(): return got.reshape(n, 3, G, n).transpose(1, 3, 0, 2).reshape(3, n * n * G)]
    unnamed x1 -> x14, local copies, waits for them, and re-layouts: 13.5 us -> 8.81 us
where the time goes in v2:
time: 109 us
  Pallas kernels  100 us (92%)
  local copies, waits for them, and re-layouts  8.81 us (8%)
    pallas_call x1, Pallas kernels, shards(): pl.pallas_call(move_kernel, out_shape=jax.ShapeDtypeStruct((chunks, n, ow...  90.8 us
    pallas_call x1, Pallas kernels, shards(): pl.pallas_call(turn_kernel, out_shape=jax.ShapeDtypeStruct((own, n * rows...  9.2 us
    unnamed x14, local copies, waits for them, and re-layouts  8.81 us

profile of v2, /device:TPU:1, one launch (start us, length us, event | category | flops | bytes accessed | tf_op | source)
XLA Modules:
  0.0 108.8 jit_solution(3691783835601598150)
XLA Ops:
  0.0 0.0 copy-start
  0.0 2.0 %copy-done = bf16[4,3,384,384]{3,2,1,0:T(8,128)(2,1)S(1)} copy-done((bf16[4,3,384,384]{3,2,1,0:T(8,128)(2,1)S(1)}, bf16[4,3,384,384]{3,2,1,0:T(8,128)(2,1)}, u32[]{:S(2)}) %copy-start) | copy-done | bytes 3538968
  2.0 0.0 copy-start.1
  2.0 1.7 %copy-done.1 = bf16[4,384,768]{2,1,0:T(8,128)(2,1)S(1)} copy-done((bf16[4,384,768]{2,1,0:T(8,128)(2,1)S(1)}, bf16[4,384,768]{2,1,0:T(8,128)(2,1)}, u32[]{:S(2)}) %copy-start.1) | copy-done | bytes 2359320
  3.7 0.0 copy-start.2
  3.7 1.7 %copy-done.2 = bf16[4,768,384]{2,1,0:T(8,128)(2,1)S(1)} copy-done((bf16[4,768,384]{2,1,0:T(8,128)(2,1)S(1)}, bf16[4,768,384]{2,1,0:T(8,128)(2,1)}, u32[]{:S(2)}) %copy-start.2) | copy-done | bytes 2359320
  5.3 0.0 copy-start.3
  5.3 1.4 %copy-done.3 = bf16[2048,384]{1,0:T(8,128)(2,1)S(1)} copy-done((bf16[2048,384]{1,0:T(8,128)(2,1)S(1)}, bf16[2048,384]{1,0:T(8,128)(2,1)}, u32[]{:S(2)}) %copy-start.3) | copy-done | bytes 1572888
  6.7 0.0 copy-start.4
  6.7 0.7 copy-done.4
  7.4 0.0 copy-start.5
  7.4 0.7 copy-done.5
  8.1 0.0 copy-start.6
  8.1 0.7 copy-done.6
  8.8 90.8 %shard_map.73.got = bf16[2,128,24,128]{3,2,1,0:T(8,128)(2,1)S(1)} custom-call(bf16[2048,384]{1,0:T(8,128)(2,1)S(1)} %copy-done.3, bf16[4,1152,384]{2,1,0:T(8,128)(2,1)S(1)} %bitcast.1, f32[4,384]{1,0:T(4,128)S(1)} %copy-done.4, f32[4,384]{1,0:T(4,128)S(1)} %copy-done.5, f32[4,384]{1,0:T(4,128)S(1)} %copy-done.6, bf16[4,384,768]{2,1,0:T(8,128)(2,1)S(1)} %copy-done.1, ...), custom_call_target="tpu_custom_call" | custom-call | tf_op jit(solution)/shard_map/pallas_call | solution.py:211
  99.6 9.2 %shard_map.74 = bf16[3,262144]{1,0:T(4,128)(2,1)} custom-call(bf16[2,128,24,128]{3,2,1,0:T(8,128)(2,1)S(1)} %shard_map.73.got), custom_call_target="tpu_custom_call" | custom-call | tf_op jit(solution)/shard_map/pallas_call | solution.py:235
Async XLA Ops:
  0.0 2.0 %copy-start = (bf16[4,3,384,384]{3,2,1,0:T(8,128)(2,1)S(1)}, bf16[4,3,384,384]{3,2,1,0:T(8,128)(2,1)}, u32[]{:S(2)}) copy-start(bf16[4,3,384,384]{3,2,1,0:T(8,128)(2,1)} %param.8) | copy-start | bytes 10616836
  2.0 1.7 %copy-start.1 = (bf16[4,384,768]{2,1,0:T(8,128)(2,1)S(1)}, bf16[4,384,768]{2,1,0:T(8,128)(2,1)}, u32[]{:S(2)}) copy-start(bf16[4,384,768]{2,1,0:T(8,128)(2,1)} %wi_hbm.1) | copy-start | bytes 7077892
  3.7 1.7 %copy-start.2 = (bf16[4,768,384]{2,1,0:T(8,128)(2,1)S(1)}, bf16[4,768,384]{2,1,0:T(8,128)(2,1)}, u32[]{:S(2)}) copy-start(bf16[4,768,384]{2,1,0:T(8,128)(2,1)} %wo_hbm.1) | copy-start | bytes 7077892
  5.3 1.4 %copy-start.3 = (bf16[2048,384]{1,0:T(8,128)(2,1)S(1)}, bf16[2048,384]{1,0:T(8,128)(2,1)}, u32[]{:S(2)}) copy-start(bf16[2048,384]{1,0:T(8,128)(2,1)} %x_hbm.1) | copy-start | bytes 4718596
  6.7 0.7 copy-start.4
  7.4 0.7 copy-start.5
  8.1 0.7 copy-start.6

commit v3 on v2

--- a/solution.py
+++ b/solution.py
@@ -10,8 +10,9 @@
 PAD = 8
 G = 8
 SEG = 16 // G
-TB = 16
+TB = 64
 STRIDE = 37
+VMEM = 63 * 1024 * 1024
 MESH = pl.DeviceIdType.MESH
 
 
@@ -174,27 +175,42 @@
         pltpu.make_async_copy(got.at[c], got.at[c], out_recv.at[c]).wait()
 
 
-def turn_kernel(got, out_ref, wide):
+def turn_kernel(got_hbm, out_hbm, got, wide, out, load_sem, out_sem):
     chunks, n = got.shape[0], got.shape[1]
     per = 128 // G
-    blocks = n // per
-    total = chunks * blocks
-    for r in range(3):
-        def one(b, carry):
-            c, g = b // blocks, lax.rem(b, blocks)
-            tile = got[c, pl.ds(g * per, per), pl.ds(r * G, G), :].reshape(128, n).astype(jnp.float32)
+    total = chunks * n // per
+    quarter = n // 4
+    loads = {}
+    for c in range(chunks):
+        for h in range(4):
+            part = c, pl.ds(h * quarter, quarter)
+            loads[c, h] = pltpu.make_async_copy(got_hbm.at[part], got.at[part], load_sem.at[c, h])
+            loads[c, h].start()
+    for b in range(total):
+        c, j = b // (n // per), b % (n // per) * per
+        if j % quarter == 0:
+            loads[c, j // quarter].wait()
+        for r in range(3):
+            tile = got[c, pl.ds(j, per), pl.ds(r * G, G), :].reshape(128, n).astype(jnp.float32)
             wide[pl.ds(b * 4 + r, n, stride=4 * total), :] = tile.T
+
+    width = total * 128
+    stores = []
+    for h in range(4):
+        def store(g, carry):
+            for k in range(4):
+                i = h * quarter + g * 4 + k
+                base = pl.multiple_of(i * total * 4, 4)
+                row = jnp.concatenate([wide[pl.ds(base + 4 * b, 4), :] for b in range(total)], axis=1)
+                out[:, pl.ds(pl.multiple_of(i * width, 128), width)] = row[:3].astype(jnp.bfloat16)
             return carry
 
-        lax.fori_loop(0, total, one, 0)
-
-    def store(i, carry):
-        base = pl.multiple_of(i * total * 4, 4)
-        row = jnp.concatenate([wide[pl.ds(base + 4 * b, 4), :] for b in range(total)], axis=1)
-        out_ref[:, pl.ds(pl.multiple_of(i * total * 128, 128), total * 128)] = row[:3].astype(jnp.bfloat16)
-        return carry
-
-    lax.fori_loop(0, n, store, 0)
+        lax.fori_loop(0, quarter // 4, store, 0)
+        part = slice(None), pl.ds(h * quarter * width, quarter * width)
+        stores.append(pltpu.make_async_copy(out.at[part], out_hbm.at[part], out_sem.at[h]))
+        stores[-1].start()
+    for copy in stores:
+        copy.wait()
 
 
 def shards(activations, conv_weight, conv_bias, conv_gain, mlp_gain, w_in, w_out):
@@ -229,16 +245,22 @@
             pltpu.SemaphoreType.DMA((chunks,)),
         ],
         compiler_params=pltpu.CompilerParams(
-            vmem_limit_bytes=40 * 1024 * 1024, collective_id=0, has_side_effects=True
+            vmem_limit_bytes=VMEM, collective_id=0, has_side_effects=True
         ),
     )(activations, taps, conv_bias, conv_gain, mlp_gain, w_in, w_out)
     return pl.pallas_call(
         turn_kernel,
         out_shape=jax.ShapeDtypeStruct((own, n * rows), jnp.bfloat16),
-        in_specs=[vm],
-        out_specs=vm,
-        scratch_shapes=[pltpu.VMEM((n * rows // 128 * 4, 128), jnp.float32)],
-        compiler_params=pltpu.CompilerParams(vmem_limit_bytes=40 * 1024 * 1024),
+        in_specs=[hbm],
+        out_specs=hbm,
+        scratch_shapes=[
+            pltpu.VMEM((chunks, n, own * G, n), jnp.bfloat16),
+            pltpu.VMEM((n * rows // 128 * 4, 128), jnp.float32),
+            pltpu.VMEM((own, n * rows), jnp.bfloat16),
+            pltpu.SemaphoreType.DMA((chunks, 4)),
+            pltpu.SemaphoreType.DMA((4,)),
+        ],
+        compiler_params=pltpu.CompilerParams(vmem_limit_bytes=VMEM),
     )(got)
 
 

time: 109 us -> 82.4 us (0.76)
  Pallas kernels: 100 us -> 82.2 us
  local copies, waits for them, and re-layouts: 8.81 us -> 0 us
    pallas_call x1, Pallas kernels: 90.8 us -> 77.3 us  [shards(): pl.pallas_call(move_kernel, out_shape=jax.ShapeDtypeStruct((chunks, n, ow...]
    unnamed x14 -> x0, local copies, waits for them, and re-layouts: 8.81 us -> none
    pallas_call x1, Pallas kernels: 9.2 us -> 4.95 us  [shards(): pl.pallas_call(turn_kernel, out_shape=jax.ShapeDtypeStruct((own, n * rows...]
where the time goes in v3:
time: 82.4 us; the launch traced here: 82.3 us
  Pallas kernels  82.2 us (100%)
    pallas_call x1, Pallas kernels, shards(): pl.pallas_call(move_kernel, out_shape=jax.ShapeDtypeStruct((chunks, n, ow...  77.3 us
    pallas_call x1, Pallas kernels, shards(): pl.pallas_call(turn_kernel, out_shape=jax.ShapeDtypeStruct((own, n * rows...  4.95 us

profile of v3, /device:TPU:1, one launch (start us, length us, event | category | flops | bytes accessed | tf_op | source)
XLA Modules:
  0.0 82.3 jit_solution(10332638778122227451)
XLA Ops:
  0.0 77.3 %shard_map.73.got_hbm = bf16[2,128,24,128]{3,2,1,0:T(8,128)(2,1)} custom-call(bf16[2048,384]{1,0:T(8,128)(2,1)} %x_hbm.1, bf16[4,1152,384]{2,1,0:T(8,128)(2,1)} %bitcast.1, f32[4,384]{1,0:T(4,128)} %cb.1, f32[4,384]{1,0:T(4,128)} %cg.1, f32[4,384]{1,0:T(4,128)} %mg.1, bf16[4,384,768]{2,1,0:T(8,128)(2,1)} %wi_hbm.1, bf16[4,768,384]{2,1,0:T(8,128)(2,1)} %wo_hbm.1), custom_call_target="tpu_custom_call" | custom-call | tf_op jit(solution)/shard_map/pallas_call | solution.py:227
  77.3 5.0 %shard_map.74 = bf16[3,262144]{1,0:T(4,128)(2,1)} custom-call(bf16[2,128,24,128]{3,2,1,0:T(8,128)(2,1)} %shard_map.73.got_hbm), custom_call_target="tpu_custom_call" | custom-call | tf_op jit(solution)/shard_map/pallas_call | solution.py:251

commit v4 on v3

v4 whole, which is shorter than its diff:
```python
import functools

import jax
import jax.numpy as jnp
from jax import lax
from jax.experimental import pallas as pl
from jax.experimental.pallas import tpu as pltpu
from jax.sharding import PartitionSpec as P

PAD = 8
G = 4
SEG = 16 // G
GROUPS = ((0,), (1, 2), (3,))
VMEM = 63 * 1024 * 1024
MESH = pl.DeviceIdType.MESH


def gelu(x):
    half = 0.5 * x
    return half + half * lax.erf(x * 0.7071067811865476)


def rms(wide, gain):
    inverse = lax.rsqrt(jnp.mean(wide * wide, axis=-1, keepdims=True) + 1e-06)
    return (wide * inverse * gain).astype(jnp.bfloat16)


def tower(group, state, normed, flat, cw, cb, cg, mg, wi, wo):
    nb, ch = state.shape[1], state.shape[-1]
    layers = cw.shape[0]
    k = len(group)
    rows = k * nb * 16
    own, subs = pl.ds(group[0], k), pl.ds(0, k)

    def load():
        return state[own].reshape(rows, ch).astype(jnp.float32)

    def put(buf, wide, gain):
        normed[buf, subs, pl.ds(PAD, nb)] = rms(wide, gain[None, :]).reshape(k, nb, 16, ch)
        tail = normed[buf, subs, pl.ds(nb, PAD)].astype(jnp.float32)
        head = normed[buf, subs, pl.ds(PAD, PAD)].astype(jnp.float32)
        zero = jnp.zeros((k, PAD, G, ch), jnp.float32)
        normed[buf, subs, pl.ds(0, PAD)] = jnp.concatenate([zero, tail[:, :, : 16 - G]], axis=2).astype(jnp.bfloat16)
        normed[buf, subs, pl.ds(PAD + nb, PAD)] = jnp.concatenate([head[:, :, G:], zero], axis=2).astype(jnp.bfloat16)

    def body(layer, last):
        cur = lax.rem(layer, 2)
        d = lax.shift_left(1, layer)
        lhs = jnp.concatenate(
            [normed[cur, subs, pl.ds(PAD + s, nb)].reshape(rows, ch) for s in (-d, 0, d)], axis=1
        )
        pre = jnp.dot(lhs, cw[layer], preferred_element_type=jnp.float32) + cb[layer, :][None, :]
        middle = (load() + gelu(pre)).astype(jnp.bfloat16)
        wide = middle.astype(jnp.float32)
        inner = rms(wide, mg[layer, :][None, :])
        hidden = gelu(jnp.dot(inner, wi[layer], preferred_element_type=jnp.float32)).astype(jnp.bfloat16)
        out = wide + jnp.dot(hidden, wo[layer], preferred_element_type=jnp.float32)
        if last:
            for j in range(ch // 128):
                flat[j, pl.ds(0, rows)] = out[:, j * 128 : (j + 1) * 128]
        else:
            new = out.astype(jnp.bfloat16)
            state[own] = new.reshape(k, nb, 16, ch)
            put(1 - cur, new.astype(jnp.float32), cg[layer + 1, :])

    def one_layer(layer, carry):
        body(layer, False)
        return carry

    put(0, load(), cg[0, :])
    lax.fori_loop(0, layers - 1, one_layer, 0)
    body(layers - 1, True)


def emit(part, base, flat, turned, packed, nb):
    pair, h = part // 2, part % 2
    for k in range(flat.shape[0]):
        for o in range(G):
            rows = [flat[k, pl.ds(base + f * G + o, nb, stride=16), :] for f in range(SEG)]
            turned[pl.ds(k * 128 * G + o, 128, stride=G), :] = jnp.concatenate(rows, axis=0).T
    own, step = packed.shape[2], 16

    def cast(g, carry):
        values = turned[pl.ds(pl.multiple_of(g * step * own * G, 8), step * own * G), :]
        packed[pair, pl.ds(g * step, step), :, pl.ds(h * G, G)] = values.astype(jnp.bfloat16).reshape(step, own, G, 128)
        return carry

    lax.fori_loop(0, packed.shape[1] // step, cast, 0)


def move_kernel(
    x_hbm, cw_hbm, cb, cg, mg, wi_hbm, wo_hbm, got,
    state, normed, flat, turned, packed, cw, wi, wo,
    load_sem, in_send, in_recv, out_send, out_recv,
):
    me = lax.axis_index("seq")
    pairs, n = packed.shape[0], packed.shape[1]
    parts, nb = state.shape[0], state.shape[1]
    loads = [
        pltpu.make_async_copy(s, d, load_sem.at[k])
        for k, (s, d) in enumerate(((cw_hbm, cw), (wi_hbm, wi), (wo_hbm, wo)))
    ]
    for load in loads:
        load.start()

    xs = [lax.rem(me // 32 + k, 4) * 32 for k in range(4)]
    cores = [lax.rem(me + k, 2) for k in range(2)]
    ends = [x + core for x in xs for core in cores]
    z_me, y_me = lax.rem(me // 8, 4), lax.rem(me // 2, 4)

    def each_peer(act):
        for end in ends[1:]:
            act(end + z_me * 8 + y_me * 2)

        def step(g, carry):
            y = lax.rem(g, 4)
            z = lax.rem(g // 4 + y, 4)
            middle = lax.rem(z_me + z, 4) * 8 + lax.rem(y_me + y, 4) * 2
            for end in ends:
                act(end + middle)
            return carry

        lax.fori_loop(1, n // len(ends), step, 0)

    barrier = pltpu.get_barrier_semaphore()
    each_peer(lambda j: pl.semaphore_signal(barrier, inc=1, device_id=(j,), device_id_type=MESH))
    pl.semaphore_wait(barrier, n - 1)

    for part in range(parts):
        pair, h = part // 2, part % 2
        place = state.at[part, lax.rem(me, nb), pl.ds(me // nb * G, G)]

        def source(j):
            return x_hbm.at[pl.ds((pair * n + j) * 2 * G + h * G, G)]

        pltpu.make_async_copy(source(me), place, in_recv.at[part]).start()
        each_peer(
            lambda j: pltpu.make_async_remote_copy(
                source(j), place, in_send.at[pair], in_recv.at[part], device_id=(j,), device_id_type=MESH
            ).start()
        )
    for load in loads:
        load.wait()

    for group in GROUPS:
        for part in group:
            pltpu.make_async_copy(state.at[part], state.at[part], in_recv.at[part]).wait()
        tower(group, state, normed, flat, cw, cb, cg, mg, wi, wo)
        for at, part in enumerate(group):
            emit(part, at * nb * 16, flat, turned, packed, nb)
            pair, rows = part // 2, pl.ds(part % 2 * G, G)
            place = got.at[pair, me, :, rows]
            pltpu.make_async_copy(packed.at[pair, me, :, rows], place, out_recv.at[pair]).start()
            each_peer(
                lambda j: pltpu.make_async_remote_copy(
                    packed.at[pair, j, :, rows], place, out_send.at[pair], out_recv.at[pair],
                    device_id=(j,), device_id_type=MESH,
                ).start()
            )

    for pair in range(pairs):
        sent = x_hbm.at[pl.ds(0, (n - 1) * 2 * G)]
        pltpu.make_async_copy(sent, sent, in_send.at[pair]).wait()
        sent = packed.at[pair, pl.ds(0, n - 1)]
        pltpu.make_async_copy(sent, sent, out_send.at[pair]).wait()
        pltpu.make_async_copy(got.at[pair], got.at[pair], out_recv.at[pair]).wait()


def turn_kernel(got_hbm, out_hbm, got, wide, out, load_sem, out_sem):
    pairs, n = got.shape[0], got.shape[1]
    rows = got.shape[3]
    per = 128 // rows
    total = pairs * n // per
    quarter = n // 4
    loads = {}
    for c in range(pairs):
        for h in range(4):
            part = c, pl.ds(h * quarter, quarter)
            loads[c, h] = pltpu.make_async_copy(got_hbm.at[part], got.at[part], load_sem.at[c, h])
            loads[c, h].start()
    for b in range(total):
        c, j = b // (n // per), b % (n // per) * per
        if j % quarter == 0:
            loads[c, j // quarter].wait()
        for r in range(3):
            tile = got[c, pl.ds(j, per), r].reshape(128, n).astype(jnp.float32)
            wide[pl.ds(b * 4 + r, n, stride=4 * total), :] = tile.T

    width = total * 128
    stores = []
    for h in range(4):
        def store(g, carry):
            for k in range(4):
                i = h * quarter + g * 4 + k
                base = pl.multiple_of(i * total * 4, 4)
                row = jnp.concatenate([wide[pl.ds(base + 4 * b, 4), :] for b in range(total)], axis=1)
                out[:, pl.ds(pl.multiple_of(i * width, 128), width)] = row[:3].astype(jnp.bfloat16)
            return carry

        lax.fori_loop(0, quarter // 4, store, 0)
        part = slice(None), pl.ds(h * quarter * width, quarter * width)
        stores.append(pltpu.make_async_copy(out.at[part], out_hbm.at[part], out_sem.at[h]))
        stores[-1].start()
    for copy in stores:
        copy.wait()


def shards(activations, conv_weight, conv_bias, conv_gain, mlp_gain, w_in, w_out):
    n = lax.axis_size("seq")
    rows, ch = activations.shape
    layers = conv_weight.shape[0]
    hid = w_in.shape[2]
    parts = rows // (n * G)
    pairs = parts // 2
    nb = n // SEG
    own = ch // n
    taps = conv_weight.reshape(layers, 3 * ch, ch)
    vm = pl.BlockSpec(memory_space=pltpu.VMEM)
    hbm = pl.BlockSpec(memory_space=pl.ANY)
    widest = max(map(len, GROUPS))
    tiles = (pairs, n, own, 2 * G, n)
    got = pl.pallas_call(
        move_kernel,
        out_shape=jax.ShapeDtypeStruct(tiles, jnp.bfloat16),
        in_specs=[hbm, hbm, vm, vm, vm, hbm, hbm],
        out_specs=hbm,
        scratch_shapes=[
            pltpu.VMEM((parts, nb, 16, ch), jnp.bfloat16),
            pltpu.VMEM((2, widest, nb + 2 * PAD, 16, ch), jnp.bfloat16),
            pltpu.VMEM((ch // 128, widest * nb * 16, 128), jnp.float32),
            pltpu.VMEM((ch * G, 128), jnp.float32),
            pltpu.VMEM(tiles, jnp.bfloat16),
            pltpu.VMEM((layers, 3 * ch, ch), jnp.bfloat16),
            pltpu.VMEM((layers, ch, hid), jnp.bfloat16),
            pltpu.VMEM((layers, hid, ch), jnp.bfloat16),
            pltpu.SemaphoreType.DMA((3,)),
            pltpu.SemaphoreType.DMA((pairs,)),
            pltpu.SemaphoreType.DMA((parts,)),
            pltpu.SemaphoreType.DMA((pairs,)),
            pltpu.SemaphoreType.DMA((pairs,)),
        ],
        compiler_params=pltpu.CompilerParams(
            vmem_limit_bytes=VMEM, collective_id=0, has_side_effects=True
        ),
    )(activations, taps, conv_bias, conv_gain, mlp_gain, w_in, w_out)
    return pl.pallas_call(
        turn_kernel,
        out_shape=jax.ShapeDtypeStruct((own, n * rows), jnp.bfloat16),
        in_specs=[hbm],
        out_specs=hbm,
        scratch_shapes=[
            pltpu.VMEM(tiles, jnp.bfloat16),
            pltpu.VMEM((n * rows // 128 * 4, 128), jnp.float32),
            pltpu.VMEM((own, n * rows), jnp.bfloat16),
            pltpu.SemaphoreType.DMA((pairs, 4)),
            pltpu.SemaphoreType.DMA((4,)),
        ],
        compiler_params=pltpu.CompilerParams(vmem_limit_bytes=VMEM),
    )(got)


def solution(mesh):
    in_specs = (P("seq", None), P(), P(), P(), P(), P(), P())
    out_specs = P("seq", None)
    return jax.shard_map(shards, mesh=mesh, in_specs=in_specs, out_specs=out_specs, check_vma=False)
```

time: 82.4 us -> 74 us (0.90)
  Pallas kernels: 82.2 us -> 73.7 us
    pallas_call x1, Pallas kernels: 77.3 us -> 68.8 us  [shards(): pl.pallas_call(move_kernel, out_shape=jax.ShapeDtypeStruct(tiles, jnp.bfl...]
where the time goes in v4:
time: 74 us; the launch traced here: 73.9 us
  Pallas kernels  73.7 us (100%)
    pallas_call x1, Pallas kernels, shards(): pl.pallas_call(move_kernel, out_shape=jax.ShapeDtypeStruct(tiles, jnp.bfl...  68.8 us
    pallas_call x1, Pallas kernels, shards(): pl.pallas_call(turn_kernel, out_shape=jax.ShapeDtypeStruct((own, n * rows...  4.95 us

profile of v4, /device:TPU:1, one launch (start us, length us, event | category | flops | bytes accessed | tf_op | source)
XLA Modules:
  0.0 73.9 jit_solution(29349879783926150)
XLA Ops:
  0.0 68.8 %shard_map.73.got_hbm = bf16[2,128,3,8,128]{4,3,2,1,0:T(8,128)(2,1)} custom-call(bf16[2048,384]{1,0:T(8,128)(2,1)} %x_hbm.1, bf16[4,1152,384]{2,1,0:T(8,128)(2,1)} %bitcast.1, f32[4,384]{1,0:T(4,128)} %cb.1, f32[4,384]{1,0:T(4,128)} %cg.1, f32[4,384]{1,0:T(4,128)} %mg.1, bf16[4,384,768]{2,1,0:T(8,128)(2,1)} %wi_hbm.1, bf16[4,768,384]{2,1,0:T(8,128)(2,1)} %wo_hbm.1), custom_call_target="tpu_custom_call" | custom-call | tf_op jit(solution)/shard_map/pallas_call | solution.py:222
  68.8 5.0 %shard_map.74 = bf16[3,262144]{1,0:T(4,128)(2,1)} custom-call(bf16[2,128,3,8,128]{4,3,2,1,0:T(8,128)(2,1)} %shard_map.73.got_hbm), custom_call_target="tpu_custom_call" | custom-call | tf_op jit(solution)/shard_map/pallas_call | solution.py:246

commit v5 on v4

v5 whole, which is shorter than its diff:
```python
import functools

import jax
import jax.numpy as jnp
from jax import lax
from jax.experimental import pallas as pl
from jax.experimental.pallas import tpu as pltpu
from jax.sharding import PartitionSpec as P

PAD = 8
PARTS = ((0, 0, 4), (1, 0, 8), (0, 4, 4))
VMEM = 63 * 1024 * 1024
MESH = pl.DeviceIdType.MESH


def gelu(x):
    half = 0.5 * x
    return half + half * lax.erf(x * 0.7071067811865476)


def rms(wide, gain):
    inverse = lax.rsqrt(jnp.mean(wide * wide, axis=-1, keepdims=True) + 1e-06)
    return (wide * inverse * gain).astype(jnp.bfloat16)


def tower(state, normed, flat, cw, cb, cg, mg, wi, wo, G):
    nb, _, ch = state.shape
    layers = cw.shape[0]
    rows = nb * 16

    def load():
        return state[...].reshape(rows, ch).astype(jnp.float32)

    def put(buf, wide, gain):
        normed[buf, pl.ds(PAD, nb)] = rms(wide, gain[None, :]).reshape(nb, 16, ch)
        tail = normed[buf, pl.ds(nb, PAD)].astype(jnp.float32)
        head = normed[buf, pl.ds(PAD, PAD)].astype(jnp.float32)
        zero = jnp.zeros((PAD, G, ch), jnp.float32)
        normed[buf, pl.ds(0, PAD)] = jnp.concatenate([zero, tail[:, : 16 - G]], axis=1).astype(jnp.bfloat16)
        normed[buf, pl.ds(PAD + nb, PAD)] = jnp.concatenate([head[:, G:], zero], axis=1).astype(jnp.bfloat16)

    def body(layer, last):
        cur = lax.rem(layer, 2)
        d = lax.shift_left(1, layer)
        lhs = jnp.concatenate([normed[cur, pl.ds(PAD + s, nb)].reshape(rows, ch) for s in (-d, 0, d)], axis=1)
        pre = jnp.dot(lhs, cw[layer], preferred_element_type=jnp.float32) + cb[layer, :][None, :]
        middle = (load() + gelu(pre)).astype(jnp.bfloat16)
        wide = middle.astype(jnp.float32)
        inner = rms(wide, mg[layer, :][None, :])
        hidden = gelu(jnp.dot(inner, wi[layer], preferred_element_type=jnp.float32)).astype(jnp.bfloat16)
        out = wide + jnp.dot(hidden, wo[layer], preferred_element_type=jnp.float32)
        if last:
            for j in range(ch // 128):
                flat[j, pl.ds(0, rows)] = out[:, j * 128 : (j + 1) * 128]
        else:
            new = out.astype(jnp.bfloat16)
            state[...] = new.reshape(nb, 16, ch)
            put(1 - cur, new.astype(jnp.float32), cg[layer + 1, :])

    def one_layer(layer, carry):
        body(layer, False)
        return carry

    put(0, load(), cg[0, :])
    lax.fori_loop(0, layers - 1, one_layer, 0)
    body(layers - 1, True)


def emit(part, flat, turned, packed, nb):
    pair, first, G = part
    for k in range(flat.shape[0]):
        for o in range(G):
            rows = [flat[k, pl.ds(f * G + o, nb, stride=16), :] for f in range(16 // G)]
            turned[pl.ds(k * 128 * G + o, 128, stride=G), :] = jnp.concatenate(rows, axis=0).T
    own, step = packed.shape[2], 64 // G

    def cast(g, carry):
        values = turned[pl.ds(pl.multiple_of(g * step * own * G, 8), step * own * G), :]
        packed[pair, pl.ds(g * step, step), :, pl.ds(first, G)] = values.astype(jnp.bfloat16).reshape(step, own, G, 128)
        return carry

    lax.fori_loop(0, packed.shape[1] // step, cast, 0)


def turn(got, wide, after=()):
    n, own, rows, _ = got.shape
    per = 128 // rows
    for b in range(n // per):
        if b < len(after):
            after[b].wait()
        for r in range(own):
            tile = got[pl.ds(b * per, per), r].reshape(128, n).astype(jnp.float32)
            wide[pl.ds(b * 4 + r, n, stride=4 * (n // per)), :] = tile.T


def turned_row(wide, i, blocks):
    base = pl.multiple_of(i * blocks * 4, 4)
    row = jnp.concatenate([wide[pl.ds(base + 4 * b, 4), :] for b in range(blocks)], axis=1)
    return row[:3].astype(jnp.bfloat16)


def move_kernel(
    x_hbm, cw_hbm, cb_hbm, cg_hbm, mg_hbm, wi_hbm, wo_hbm, got, half_hbm,
    state_a, state_b, state_c, normed, flat, turned, packed, got_b, wide, half, cw, cb, cg, mg, wi, wo,
    load_sem, in_send, in_recv, out_send, out_recv, half_sem,
):
    me = lax.axis_index("seq")
    n = packed.shape[1]
    states = state_a, state_b, state_c
    loads = [
        pltpu.make_async_copy(s, d, load_sem.at[k])
        for k, (s, d) in enumerate(
            ((cw_hbm, cw), (cb_hbm, cb), (cg_hbm, cg), (mg_hbm, mg), (wi_hbm, wi), (wo_hbm, wo))
        )
    ]
    for load in loads:
        load.start()

    xs = [lax.rem(me // 32 + k, 4) * 32 for k in range(4)]
    cores = [lax.rem(me + k, 2) for k in range(2)]
    ends = [x + core for x in xs for core in cores]
    z_me, y_me = lax.rem(me // 8, 4), lax.rem(me // 2, 4)

    def each_peer(act):
        for end in ends[1:]:
            act(end + z_me * 8 + y_me * 2)

        def step(g, carry):
            y = lax.rem(g, 4)
            z = lax.rem(g // 4 + y, 4)
            middle = lax.rem(z_me + z, 4) * 8 + lax.rem(y_me + y, 4) * 2
            for end in ends:
                act(end + middle)
            return carry

        lax.fori_loop(1, n // len(ends), step, 0)

    barrier = pltpu.get_barrier_semaphore()
    each_peer(lambda j: pl.semaphore_signal(barrier, inc=1, device_id=(j,), device_id_type=MESH))
    pl.semaphore_wait(barrier, n - 1)

    for k, (pair, first, G) in enumerate(PARTS):
        nb = states[k].shape[0]
        place = states[k].at[lax.rem(me, nb), pl.ds(me // nb * G, G)]

        def source(j):
            return x_hbm.at[pl.ds((pair * n + j) * 8 + first, G)]

        pltpu.make_async_copy(source(me), place, in_recv.at[k]).start()
        each_peer(
            lambda j: pltpu.make_async_remote_copy(
                source(j), place, in_send.at[pair], in_recv.at[k], device_id=(j,), device_id_type=MESH
            ).start()
        )
    for load in loads:
        load.wait()

    for k, part in enumerate(PARTS):
        pair, first, G = part
        state = states[k]
        pltpu.make_async_copy(state, state, in_recv.at[k]).wait()
        tower(state, normed, flat, cw, cb, cg, mg, wi, wo, G)
        emit(part, flat, turned, packed, state.shape[0])
        rows = pl.ds(first, G)
        place = (got_b if pair else got).at[me, :, rows]
        pltpu.make_async_copy(packed.at[pair, me, :, rows], place, out_recv.at[pair]).start()
        each_peer(
            lambda j: pltpu.make_async_remote_copy(
                packed.at[pair, j, :, rows], place, out_send.at[pair], out_recv.at[pair],
                device_id=(j,), device_id_type=MESH,
            ).start()
        )

    pltpu.make_async_copy(got_b, got_b, out_recv.at[1]).wait()
    turn(got_b, wide)
    blocks = n // 16
    width = blocks * 128

    def store(g, carry):
        for k in range(4):
            i = g * 4 + k
            half[:, pl.ds(pl.multiple_of(i * width, 128), width)] = turned_row(wide, i, blocks)
        return carry

    lax.fori_loop(0, n // 4, store, 0)
    out = pltpu.make_async_copy(half, half_hbm, half_sem)
    out.start()
    for pair in range(2):
        sent = x_hbm.at[pl.ds(0, (n - 1) * 8)]
        pltpu.make_async_copy(sent, sent, in_send.at[pair]).wait()
        sent = packed.at[pair, pl.ds(0, n - 1)]
        pltpu.make_async_copy(sent, sent, out_send.at[pair]).wait()
    out.wait()
    pltpu.make_async_copy(got, got, out_recv.at[0]).wait()


def turn_kernel(got_hbm, half_hbm, out_hbm, got, half, wide, out, load_sem, half_sem, out_sem):
    n = got.shape[0]
    quarter = n // 4
    loads = []
    for b in range(8):
        part = pl.ds(b * 16, 16)
        loads.append(pltpu.make_async_copy(got_hbm.at[part], got.at[part], load_sem.at[b]))
        loads[-1].start()
    other = pltpu.make_async_copy(half_hbm, half, half_sem)
    other.start()
    turn(got, wide, loads)
    other.wait()
    blocks = n // 16
    width = blocks * 128
    stores = []
    for h in range(4):
        def store(g, carry):
            for k in range(4):
                i = h * quarter + g * 4 + k
                base = pl.multiple_of(i * 2 * width, 128)
                out[:, pl.ds(base, width)] = turned_row(wide, i, blocks)
                out[:, pl.ds(base + width, width)] = half[:, pl.ds(pl.multiple_of(i * width, 128), width)]
            return carry

        lax.fori_loop(0, quarter // 4, store, 0)
        part = slice(None), pl.ds(h * quarter * 2 * width, quarter * 2 * width)
        stores.append(pltpu.make_async_copy(out.at[part], out_hbm.at[part], out_sem.at[h]))
        stores[-1].start()
    for copy in stores:
        copy.wait()


def shards(activations, conv_weight, conv_bias, conv_gain, mlp_gain, w_in, w_out):
    n = lax.axis_size("seq")
    rows, ch = activations.shape
    layers = conv_weight.shape[0]
    hid = w_in.shape[2]
    own = ch // n
    taps = conv_weight.reshape(layers, 3 * ch, ch)
    hbm = pl.BlockSpec(memory_space=pl.ANY)
    states = [pltpu.VMEM((n * G // 16, 16, ch), jnp.bfloat16) for _, _, G in PARTS]
    tiles = pltpu.VMEM((n, own, 8, n), jnp.bfloat16)
    wide = pltpu.VMEM((n * n // 16 * 4, 128), jnp.float32)
    half = pltpu.VMEM((own, n * rows // 2), jnp.bfloat16)
    small = pltpu.VMEM((layers, ch), jnp.float32)
    dma = pltpu.SemaphoreType.DMA
    got, second = pl.pallas_call(
        move_kernel,
        out_shape=[
            jax.ShapeDtypeStruct((n, own, 8, n), jnp.bfloat16),
            jax.ShapeDtypeStruct((own, n * rows // 2), jnp.bfloat16),
        ],
        in_specs=[hbm] * 7,
        out_specs=[hbm] * 2,
        scratch_shapes=states
        + [
            pltpu.VMEM((2, n // 2 + 2 * PAD, 16, ch), jnp.bfloat16),
            pltpu.VMEM((ch // 128, n * 8, 128), jnp.float32),
            pltpu.VMEM((ch * 8, 128), jnp.float32),
            pltpu.VMEM((2, n, own, 8, n), jnp.bfloat16),
            tiles,
            wide,
            half,
            pltpu.VMEM((layers, 3 * ch, ch), jnp.bfloat16),
            small,
            small,
            small,
            pltpu.VMEM((layers, ch, hid), jnp.bfloat16),
            pltpu.VMEM((layers, hid, ch), jnp.bfloat16),
            dma((6,)),
            dma((2,)),
            dma((3,)),
            dma((2,)),
            dma((2,)),
            dma,
        ],
        compiler_params=pltpu.CompilerParams(
            vmem_limit_bytes=VMEM, collective_id=0, has_side_effects=True
        ),
    )(activations, taps, conv_bias, conv_gain, mlp_gain, w_in, w_out)
    return pl.pallas_call(
        turn_kernel,
        out_shape=jax.ShapeDtypeStruct((own, n * rows), jnp.bfloat16),
        in_specs=[hbm] * 2,
        out_specs=hbm,
        scratch_shapes=[
            tiles,
            half,
            wide,
            pltpu.VMEM((own, n * rows), jnp.bfloat16),
            dma((8,)),
            dma,
            dma((4,)),
        ],
        compiler_params=pltpu.CompilerParams(vmem_limit_bytes=VMEM),
    )(got, second)


def solution(mesh):
    in_specs = (P("seq", None), P(), P(), P(), P(), P(), P())
    out_specs = P("seq", None)
    return jax.shard_map(shards, mesh=mesh, in_specs=in_specs, out_specs=out_specs, check_vma=False)
```

time: 74 us -> 70.2 us (0.949)
  Pallas kernels: 73.7 us -> 69.9 us
    pallas_call x1, Pallas kernels: 68.8 us -> 65.9 us  [shards(): pl.pallas_call(move_kernel, out_shape=[jax.ShapeDtypeStruct((n, own, 8, n...]
    pallas_call x1, Pallas kernels: 4.95 us -> 4.05 us  [shards(): pl.pallas_call(turn_kernel, out_shape=jax.ShapeDtypeStruct((own, n * rows...]
where the time goes in v5:
time: 70.2 us; the launch traced here: 70.1 us
  Pallas kernels  69.9 us (100%)
    pallas_call x1, Pallas kernels, shards(): pl.pallas_call(move_kernel, out_shape=[jax.ShapeDtypeStruct((n, own, 8, n...  65.9 us
    pallas_call x1, Pallas kernels, shards(): pl.pallas_call(turn_kernel, out_shape=jax.ShapeDtypeStruct((own, n * rows...  4.05 us

profile of v5, /device:TPU:1, one launch (start us, length us, event | category | flops | bytes accessed | tf_op | source)
XLA Modules:
  0.0 70.1 jit_solution(1323151598335126384)
XLA Ops:
  0.0 65.9 %shard_map.73 = (bf16[128,3,8,128]{3,2,1,0:T(8,128)(2,1)}, bf16[3,131072]{1,0:T(4,128)(2,1)}) custom-call(bf16[2048,384]{1,0:T(8,128)(2,1)} %x_hbm.1, bf16[4,1152,384]{2,1,0:T(8,128)(2,1)} %bitcast.1, f32[4,384]{1,0:T(4,128)} %cb_hbm.1, f32[4,384]{1,0:T(4,128)} %cg_hbm.1, f32[4,384]{1,0:T(4,128)} %mg_hbm.1, bf16[4,384,768]{2,1,0:T(8,128)(2,1)} %wi_hbm.1, ...), custom_call_target="tpu_custom_call" | custom-call | tf_op jit(solution)/shard_map/pallas_call | solution.py:243
  65.9 4.1 %shard_map.74 = bf16[3,262144]{1,0:T(4,128)(2,1)} custom-call(bf16[128,3,8,128]{3,2,1,0:T(8,128)(2,1)} %get-tuple-element.7.got_hbm, bf16[3,131072]{1,0:T(4,128)(2,1)} %get-tuple-element.8.half_hbm), custom_call_target="tpu_custom_call" | custom-call | tf_op jit(solution)/shard_map/pallas_call | solution.py:277

commit v6 on v5

--- a/solution.py
+++ b/solution.py
@@ -135,6 +135,17 @@
 
         lax.fori_loop(1, n // len(ends), step, 0)
 
+    zs = [lax.rem(z_me + k, 4) * 8 for k in range(4)]
+    ys = [lax.rem(y_me + k, 4) * 2 for k in range(4)]
+    hops = (0, 1, 2, 1)
+    steps = [(x, y, z, c) for y in range(4) for z in range(4) for x in range(4) for c in range(2)][1:]
+    steps.sort(key=lambda s: -hops[s[0]] - hops[s[1]] - hops[s[2]])
+    middles = {(y, z): ys[y] + zs[z] for y in range(4) for z in range(4)}
+
+    def far_first(act):
+        for x, y, z, c in steps:
+            act(ends[x * 2 + c] + middles[y, z])
+
     barrier = pltpu.get_barrier_semaphore()
     each_peer(lambda j: pl.semaphore_signal(barrier, inc=1, device_id=(j,), device_id_type=MESH))
     pl.semaphore_wait(barrier, n - 1)
@@ -147,7 +158,7 @@
             return x_hbm.at[pl.ds((pair * n + j) * 8 + first, G)]
 
         pltpu.make_async_copy(source(me), place, in_recv.at[k]).start()
-        each_peer(
+        (far_first if k == 0 else each_peer)(
             lambda j: pltpu.make_async_remote_copy(
                 source(j), place, in_send.at[pair], in_recv.at[k], device_id=(j,), device_id_type=MESH
             ).start()
@@ -164,7 +175,7 @@
         rows = pl.ds(first, G)
         place = (got_b if pair else got).at[me, :, rows]
         pltpu.make_async_copy(packed.at[pair, me, :, rows], place, out_recv.at[pair]).start()
-        each_peer(
+        (far_first if k == len(PARTS) - 1 else each_peer)(
             lambda j: pltpu.make_async_remote_copy(
                 packed.at[pair, j, :, rows], place, out_send.at[pair], out_recv.at[pair],
                 device_id=(j,), device_id_type=MESH,

time: 70.2 us -> 68.5 us (0.976)
  Pallas kernels: 69.9 us -> 68.2 us
    pallas_call x1, Pallas kernels: 65.9 us -> 64.2 us  [shards(): pl.pallas_call(move_kernel, out_shape=[jax.ShapeDtypeStruct((n, own, 8, n...]
where the time goes in v6:
time: 68.5 us; the launch traced here: 68.4 us
  Pallas kernels  68.2 us (100%)
    pallas_call x1, Pallas kernels, shards(): pl.pallas_call(move_kernel, out_shape=[jax.ShapeDtypeStruct((n, own, 8, n...  64.2 us
    pallas_call x1, Pallas kernels, shards(): pl.pallas_call(turn_kernel, out_shape=jax.ShapeDtypeStruct((own, n * rows...  4.05 us

profile of v6, /device:TPU:1, one launch (start us, length us, event | category | flops | bytes accessed | tf_op | source)
XLA Modules:
  0.0 68.4 jit_solution(11136784989099173722)
XLA Ops:
  0.0 64.2 %shard_map.73 = (bf16[128,3,8,128]{3,2,1,0:T(8,128)(2,1)}, bf16[3,131072]{1,0:T(4,128)(2,1)}) custom-call(bf16[2048,384]{1,0:T(8,128)(2,1)} %x_hbm.1, bf16[4,1152,384]{2,1,0:T(8,128)(2,1)} %bitcast.1, f32[4,384]{1,0:T(4,128)} %cb_hbm.1, f32[4,384]{1,0:T(4,128)} %cg_hbm.1, f32[4,384]{1,0:T(4,128)} %mg_hbm.1, bf16[4,384,768]{2,1,0:T(8,128)(2,1)} %wi_hbm.1, ...), custom_call_target="tpu_custom_call" | custom-call | tf_op jit(solution)/shard_map/pallas_call | solution.py:254
  64.2 4.1 %shard_map.74 = bf16[3,262144]{1,0:T(4,128)(2,1)} custom-call(bf16[128,3,8,128]{3,2,1,0:T(8,128)(2,1)} %get-tuple-element.7.got_hbm, bf16[3,131072]{1,0:T(4,128)(2,1)} %get-tuple-element.8.half_hbm), custom_call_target="tpu_custom_call" | custom-call | tf_op jit(solution)/shard_map/pallas_call | solution.py:288
